TPU v7x, 256 devices: a whole 4x4x8 slice. The times are simulated.
256 devices in a mesh: row: 16 (over x_lo, y, core), col: 16 (over x_hi, z).
Axes of the slice: x: 4 (x_hi: 2, x_lo: 2; x = x_hi * 2 + x_lo), y: 4, z: 8, core: 2. Of those that a mesh axis runs over, the one named last changes fastest.
Arguments:
- node_features: bfloat16 [65536, 256], P(('row', 'col')), may hold values from -6 to 6
- tile_values: bfloat16 [16, 16, 128, 128, 128], P('row', 'col'), may hold values from -0.09375 to 0.09375
- tile_coords: int32 [16, 16, 128, 2], P('row', 'col'), may hold values from 0 to 31, as said below
- tile_counts: int32 [16, 16], P('row', 'col'), may hold values from 32 to 128, as said below
- first_weight: bfloat16 [256, 256], replicated, may hold values from -0.375 to 0.375
- second_weight: bfloat16 [256, 128], replicated, may hold values from -0.375 to 0.375
- out_grad: bfloat16 [65536, 128], P(('row', 'col')), may hold values from -6 to 6
Outputs:
- output: bfloat16 [65536, 128], P(('row', 'col'))
- first_grad: float32 [256, 256], replicated
- second_grad: float32 [256, 128], replicated
Inputs may be any that keep to these rules, and one draw needn't show every extreme that they name: `tile_counts`: each grid cell uses at least 32 slots; at least one grid cell uses all 128 in every draw. `tile_coords`: the first entry is a tile row below 32, the second a tile column below 32; within one grid cell no two slots share a position.
All inputs are finite; a program needn't handle non-finite values.
Results may differ from a plain program's by a relative error of at most 0.005.
Values may be sent and summed in bfloat16 or wider, within the bound.
A program may use at most 64 MiB of HBM per device.

v0:
```python
import math
import jax
import jax.numpy as jnp
from jax import lax
from jax.sharding import PartitionSpec as P

HIGHEST = lax.Precision.HIGHEST


def tile_sum(tile_block, dest_index, source_index, live_slots, source, dest_tiles, flipped):
    slot_count = tile_block.shape[0]
    group_size = math.gcd(slot_count, 32)
    round_count = slot_count // group_size
    edge_size = tile_block.shape[1]
    width_size = source.shape[-1]
    grouped_tiles = tile_block.reshape(round_count, group_size, edge_size, edge_size)
    grouped_dest = dest_index.reshape(round_count, group_size)
    grouped_source = source_index.reshape(round_count, group_size)
    grouped_live = live_slots.reshape(round_count, group_size)
    target_ids = jnp.arange(dest_tiles, dtype=jnp.int32)
    einsum_form = "tba,tbw->taw" if flipped else "tab,tbw->taw"

    def add_group(running, pieces):
        group_tiles, group_dest, group_source, group_live = pieces
        picked = jnp.take(source, group_source, axis=0)
        products = jnp.einsum(einsum_form, group_tiles, picked, preferred_element_type=jnp.float32)
        select = ((group_dest[:, None] == target_ids[None, :]) & group_live[:, None]).astype(
            jnp.float32
        )
        running = running + jnp.einsum("tr,taw->raw", select, products, precision=HIGHEST)
        return (running, None)

    start_sum = jnp.zeros((dest_tiles, edge_size, width_size), jnp.float32)
    running, unused = lax.scan(
        add_group, start_sum, (grouped_tiles, grouped_dest, grouped_source, grouped_live)
    )
    return running.reshape(dest_tiles * edge_size, width_size)


def on_device(
    node_features, tile_values, tile_coords, tile_counts, first_weight, second_weight, out_grad
):
    node_rows = node_features.shape[0]
    edge_size = tile_values.shape[-1]
    slot_count = tile_values.shape[2]
    grid_rows = lax.axis_size("row")
    grid_cols = lax.axis_size("col")
    row_tiles = grid_rows * node_rows // edge_size
    col_tiles = grid_cols * node_rows // edge_size
    tile_block = tile_values.reshape(slot_count, edge_size, edge_size)
    flat_coords = tile_coords.reshape(slot_count, 2)
    tile_row = flat_coords[:, 0]
    tile_col = flat_coords[:, 1]
    live_slots = jnp.arange(slot_count, dtype=jnp.int32) < tile_counts.reshape(())
    gathered_x = lax.all_gather(node_features, "col", axis=0, tiled=True)
    feature_part = tile_sum(
        tile_block,
        tile_row,
        tile_col,
        live_slots,
        gathered_x.reshape(col_tiles, edge_size, -1),
        row_tiles,
        False,
    )
    first_mean = lax.psum_scatter(feature_part, "row", scatter_dimension=0, tiled=True)
    first_pre = jnp.dot(first_mean, first_weight.astype(jnp.float32), precision=HIGHEST)
    hidden_act = jax.nn.silu(first_pre).astype(jnp.bfloat16)
    second_wide = second_weight.astype(jnp.float32)
    gathered_h = lax.all_gather(hidden_act, "col", axis=0, tiled=True)
    hidden_part = tile_sum(
        tile_block,
        tile_row,
        tile_col,
        live_slots,
        gathered_h.reshape(col_tiles, edge_size, -1),
        row_tiles,
        False,
    )
    second_mean = lax.psum_scatter(hidden_part, "row", scatter_dimension=0, tiled=True)
    logit_rows = jnp.dot(second_mean, second_wide, precision=HIGHEST)
    output = logit_rows.astype(jnp.bfloat16)
    gathered_g = lax.all_gather(out_grad, "row", axis=0, tiled=True)
    grad_part = tile_sum(
        tile_block,
        tile_col,
        tile_row,
        live_slots,
        gathered_g.reshape(row_tiles, edge_size, -1),
        col_tiles,
        True,
    )
    back_sum = lax.psum_scatter(grad_part, "col", scatter_dimension=0, tiled=True)
    scale = 1.0 / math.sqrt(node_rows * grid_rows * grid_cols)
    second_local = jnp.dot(hidden_act.astype(jnp.float32).T, back_sum, precision=HIGHEST) * scale
    hidden_grad = jnp.dot(back_sum, second_wide.T, precision=HIGHEST)
    sigma = jax.nn.sigmoid(first_pre)
    pre_grad = hidden_grad * (sigma * (1.0 + first_pre * (1.0 - sigma)))
    second_grad = lax.psum(second_local, ("row", "col"))
    first_local = jnp.dot(first_mean.T, pre_grad, precision=HIGHEST) * scale
    first_grad = lax.psum(first_local, ("row", "col"))
    return (output, first_grad, second_grad)


def solution(mesh):
    return jax.shard_map(
        on_device,
        mesh=mesh,
        in_specs=(
            P(("row", "col"), None),
            P("row", "col", None, None, None),
            P("row", "col", None, None),
            P("row", "col"),
            P(),
            P(),
            P(("row", "col"), None),
        ),
        out_specs=(P(("row", "col"), None), P(), P()),
        check_vma=False,
    )
```

profile of v0, /device:TPU:1, one launch (start us, length us, event | category | flops | bytes accessed | tf_op | source)
XLA Modules:
  0.0 898.8 jit_solution(9143985936863349914)
XLA Ops:
  7.2 0.7 all-gather.4.cloned.1.call-update
  8.0 0.8 slice_reduce_fusion
  8.7 0.1 reshape_squeeze.4
  8.8 0.1 reshape_squeeze.5
  9.6 86.8 %all-gather.4.cloned.1.call-done = bf16[4096,256]{1,0:T(8,128)(2,1)} async-done(((bf16[256,256]{1,0:T(8,128)(2,1)}), bf16[4096,256]{1,0:T(8,128)(2,1)}) %all-gather.4.cloned.1.call-update) | async-done | bytes 2097168 | tf_op jit(solution)/shard_map/all_gather | solution.py:55
  96.3 64.7 %while.33 = (s32[]{:T(128)}, f32[32,128,256]{2,0,1:T(8,128)}, s32[4,32]{1,0:T(4,128)S(1)}, pred[4,32]{1,0:T(4,128)(4,1)S(1)}, bf16[4,32,128,128]{3,2,1,0:T(8,128...) while((s32[]{:T(128)}, f32[32,128,256]{2,0,1:T(8,128)}, ...), condition=%wide.region_1.3_spmd.clone, body=%wide.region_0.2_spmd.clone.sunk | while | flops 674237632 | bytes 24123028 | solution.py:34
  96.4 2.3 gather_fusion
  98.6 4.0 fusion.96
  102.6 8.9 select_add_fusion.6
  111.6 2.3 gather_fusion
  113.9 4.0 fusion.96
  117.9 10.2 %select_add_fusion.6 = f32[32,128,256]{2,0,1:T(8,128)} fusion(f32[32,128,256]{2,0,1:T(8,128)} %get-tuple-element.410, f32[32,128,256]{2,1,0:T(8,128)} %fusion.96, pred[]{:T(512)S(6)} %compare.9, s32[32]{0:T(128)S(1)} %fusion.97, pred[32]{0:T(512)(128)(4,1)S(1)} %dynamic-slice_bitcast_fusion.6), kind=kOutput, calls=%fused_computation.33.clone.1 | convolution fusion | flops 404752384 | bytes 12583073 | tf_op jit(solution)/shard_map/while/body/eval_jaxpr/tr,taw->raw/dot_general | solution.py:30
  128.1 2.3 gather_fusion
  130.4 4.0 fusion.96
  134.4 10.2 %select_add_fusion.6 = f32[32,128,256]{2,0,1:T(8,128)} fusion(f32[32,128,256]{2,0,1:T(8,128)} %get-tuple-element.410, f32[32,128,256]{2,1,0:T(8,128)} %fusion.96, pred[]{:T(512)S(6)} %compare.9, s32[32]{0:T(128)S(1)} %fusion.97, pred[32]{0:T(512)(128)(4,1)S(1)} %dynamic-slice_bitcast_fusion.6), kind=kOutput, calls=%fused_computation.33.clone.1 | convolution fusion | flops 404752384 | bytes 12583073 | tf_op jit(solution)/shard_map/while/body/eval_jaxpr/tr,taw->raw/dot_general | solution.py:30
  144.6 2.3 gather_fusion
  146.9 4.0 fusion.96
  150.9 10.2 %select_add_fusion.6 = f32[32,128,256]{2,0,1:T(8,128)} fusion(f32[32,128,256]{2,0,1:T(8,128)} %get-tuple-element.410, f32[32,128,256]{2,1,0:T(8,128)} %fusion.96, pred[]{:T(512)S(6)} %compare.9, s32[32]{0:T(128)S(1)} %fusion.97, pred[32]{0:T(512)(128)(4,1)S(1)} %dynamic-slice_bitcast_fusion.6), kind=kOutput, calls=%fused_computation.33.clone.1 | convolution fusion | flops 404752384 | bytes 12583073 | tf_op jit(solution)/shard_map/while/body/eval_jaxpr/tr,taw->raw/dot_general | solution.py:30
  161.0 6.6 copy.10
  167.7 0.0 all-gather.8.cloned.1.call-start
  167.7 0.7 all-gather.8.cloned.1.call-update
  168.5 65.5 %reduce-scatter.4.cloned.1.call-done = f32[256,256]{1,0:T(8,128)} async-done(((f32[4096,256]{1,0:T(8,128)}), f32[256,256]{1,0:T(8,128)}) %reduce-scatter.4.cloned.1.call-update) | async-done | bytes 262160 | tf_op jit(solution)/shard_map/reduce_scatter | solution.py:65
  234.0 1.9 multiply_convert_fusion
  235.9 0.2 reduce-scatter.8.cloned.1.call-start
  236.2 37.0 %all-gather.8.cloned.1.call-done = bf16[4096,128]{1,0:T(8,128)(2,1)} async-done(((bf16[256,128]{1,0:T(8,128)(2,1)}), bf16[4096,128]{1,0:T(8,128)(2,1)}) %all-gather.8.cloned.1.call-update) | async-done | bytes 1048592 | tf_op jit(solution)/shard_map/all_gather | solution.py:82
  273.2 35.7 %while.35 = (s32[]{:T(128)}, f32[32,128,128]{2,0,1:T(8,128)}, s32[4,32]{1,0:T(4,128)S(1)}, pred[4,32]{1,0:T(4,128)(4,1)S(1)}, bf16[4,32,128,128]{3,2,1,0:T(8,128...) while((s32[]{:T(128)}, f32[32,128,128]{2,0,1:T(8,128)}, ...), condition=%wide.region_7.9_spmd.clone, body=%wide.region_6.8_spmd.clone.sunk | while | flops 337120544 | bytes 12588823 | solution.py:34
  273.2 2.0 gather_fusion.2
  275.2 1.8 fusion.109
  277.0 3.9 select_add_fusion.8
  280.9 2.0 gather_fusion.2
  282.9 1.8 fusion.109
  284.7 5.4 select_add_fusion.8
  290.2 2.0 gather_fusion.2
  292.2 1.8 fusion.109
  294.0 5.5 select_add_fusion.8
  299.5 2.0 gather_fusion.2
  301.5 1.8 fusion.109
  303.4 5.5 select_add_fusion.8
  308.8 4.2 copy.12
  313.0 44.8 %all-gather.6.cloned.1.call-done = bf16[4096,256]{1,0:T(8,128)(2,1)} async-done(((bf16[256,256]{1,0:T(8,128)(2,1)}), bf16[4096,256]{1,0:T(8,128)(2,1)}) %all-gather.6.cloned.1.call-update) | async-done | bytes 2097168 | tf_op jit(solution)/shard_map/all_gather | solution.py:69
  357.8 65.0 %while.34 = (s32[]{:T(128)}, f32[32,128,256]{2,0,1:T(8,128)}, s32[4,32]{1,0:T(4,128)S(1)}, pred[4,32]{1,0:T(4,128)(4,1)S(1)}, bf16[4,32,128,128]{3,2,1,0:T(8,128...) while((s32[]{:T(128)}, f32[32,128,256]{2,0,1:T(8,128)}, ...), condition=%wide.region_4.6_spmd.clone, body=%wide.region_3.5_spmd.clone.sunk | while | flops 674237632 | bytes 24123028 | solution.py:34
  357.8 2.3 gather_fusion.1
  360.1 4.0 fusion.102
  364.1 8.9 select_add_fusion.7
  373.1 2.4 gather_fusion.1
  375.4 4.0 fusion.102
  379.4 10.2 %select_add_fusion.7 = f32[32,128,256]{2,0,1:T(8,128)} fusion(f32[32,128,256]{2,0,1:T(8,128)} %get-tuple-element.437, f32[32,128,256]{2,1,0:T(8,128)} %fusion.102, pred[]{:T(512)S(6)} %compare.10, s32[32]{0:T(128)S(1)} %fusion.103, pred[32]{0:T(512)(128)(4,1)S(1)} %dynamic-slice_bitcast_fusion.7), kind=kOutput, calls=%fused_computation.57.clone.1 | convolution fusion | flops 404752384 | bytes 12583073 | tf_op jit(solution)/shard_map/while/body/eval_jaxpr/tr,taw->raw/dot_general | solution.py:30
  389.7 2.3 gather_fusion.1
  392.0 4.0 fusion.102
  396.0 10.3 %select_add_fusion.7 = f32[32,128,256]{2,0,1:T(8,128)} fusion(f32[32,128,256]{2,0,1:T(8,128)} %get-tuple-element.437, f32[32,128,256]{2,1,0:T(8,128)} %fusion.102, pred[]{:T(512)S(6)} %compare.10, s32[32]{0:T(128)S(1)} %fusion.103, pred[32]{0:T(512)(128)(4,1)S(1)} %dynamic-slice_bitcast_fusion.7), kind=kOutput, calls=%fused_computation.57.clone.1 | convolution fusion | flops 404752384 | bytes 12583073 | tf_op jit(solution)/shard_map/while/body/eval_jaxpr/tr,taw->raw/dot_general | solution.py:30
  406.3 2.3 gather_fusion.1
  408.6 4.0 fusion.102
  412.6 10.2 %select_add_fusion.7 = f32[32,128,256]{2,0,1:T(8,128)} fusion(f32[32,128,256]{2,0,1:T(8,128)} %get-tuple-element.437, f32[32,128,256]{2,1,0:T(8,128)} %fusion.102, pred[]{:T(512)S(6)} %compare.10, s32[32]{0:T(128)S(1)} %fusion.103, pred[32]{0:T(512)(128)(4,1)S(1)} %dynamic-slice_bitcast_fusion.7), kind=kOutput, calls=%fused_computation.57.clone.1 | convolution fusion | flops 404752384 | bytes 12583073 | tf_op jit(solution)/shard_map/while/body/eval_jaxpr/tr,taw->raw/dot_general | solution.py:30
  422.8 6.6 copy.11
  429.4 0.0 all-reduce.3.cloned.1.call-start
  429.5 131.3 %reduce-scatter.8.cloned.1.call-done = f32[256,128]{1,0:T(8,128)} async-done(((f32[4096,128]{1,0:T(8,128)}), f32[256,128]{1,0:T(8,128)}) %reduce-scatter.8.cloned.1.call-update) | async-done | bytes 131088 | tf_op jit(solution)/shard_map/reduce_scatter | solution.py:92
  560.8 1.9 convolution_multiply_fusion.2
  562.7 1.2 convolution_multiply_fusion.1
  563.9 1.3 convolution_multiply_fusion
  565.2 67.1 %reduce-scatter.6.cloned.1.call-done = f32[256,256]{1,0:T(8,128)} async-done(((f32[4096,256]{1,0:T(8,128)}), f32[256,256]{1,0:T(8,128)}) %reduce-scatter.6.cloned.1.call-update) | async-done | bytes 262160 | tf_op jit(solution)/shard_map/reduce_scatter | solution.py:79
  632.3 1.9 convolution_convert_fusion
  634.2 254.5 %all-reduce.3.cloned.1.call-done = (f32[256,256]{1,0:T(8,128)}, f32[256,128]{1,0:T(8,128)}) async-done(((f32[256,256]{1,0:T(8,128)}, f32[256,128]{1,0:T(8,128)}), (f32[256,256]{1,0:T(8,128)}, f32[256,128]{1,0:T(8,128)})) %all-reduce.3.cloned.1.call-update) | async-done | bytes 393232 | tf_op jit(solution)/shard_map/psum | solution.py:100
  888.7 1.7 copy.55
  890.4 1.6 copy.56
  (73 shorter events, 0.7 us)
Async XLA Ops:
  7.2 226.8 %copy-start = (bf16[256,256]{1,0:T(8,128)(2,1)S(1)}, bf16[256,256]{1,0:T(8,128)(2,1)}, u32[]{:S(2)}) copy-start(bf16[256,256]{1,0:T(8,128)(2,1)} %param.19) | copy-start | bytes 393220
  7.2 89.2 %all-gather.4.cloned.1.call-start = ((), (), s32[]{:S(2)}) async-start(), calls=%async_computation.3 | async-start | bytes 2228224 | tf_op jit(solution)/shard_map/all_gather | solution.py:55
  7.9 226.1 %reduce-scatter.4.cloned.1.call-start = ((), (), s32[]{:S(2)}) async-start(), calls=%async_computation.4 | async-start | bytes 4456448 | tf_op jit(solution)/shard_map/reduce_scatter | solution.py:65
  167.7 105.5 %all-gather.8.cloned.1.call-start = ((), (), s32[]{:S(2)}) async-start(), calls=%async_computation.7 | async-start | bytes 1114112 | tf_op jit(solution)/shard_map/all_gather | solution.py:82
  168.4 189.4 %all-gather.6.cloned.1.call-start = ((), (), s32[]{:S(2)}) async-start(), calls=%async_computation.5 | async-start | bytes 2228224 | tf_op jit(solution)/shard_map/all_gather | solution.py:69
  235.9 324.9 %reduce-scatter.8.cloned.1.call-start = ((), (), s32[]{:S(2)}) async-start(), calls=%async_computation.8 | async-start | bytes 2228224 | tf_op jit(solution)/shard_map/reduce_scatter | solution.py:92
  313.0 319.3 %reduce-scatter.6.cloned.1.call-start = ((), (), s32[]{:S(2)}) async-start(), calls=%async_computation.6 | async-start | bytes 4456448 | tf_op jit(solution)/shard_map/reduce_scatter | solution.py:79
  429.4 131.4 %copy-start.1 = (bf16[256,256]{1,0:T(8,128)(2,1)S(1)}, bf16[256,256]{1,0:T(8,128)(2,1)}, u32[]{:S(2)}) copy-start(bf16[256,256]{1,0:T(8,128)(2,1)} %get-tuple-element.261) | copy-start | bytes 393220
  429.4 133.3 %copy-start.3 = (bf16[256,128]{1,0:T(8,128)(2,1)S(1)}, bf16[256,128]{1,0:T(8,128)(2,1)}, u32[]{:S(2)}) copy-start(bf16[256,128]{1,0:T(8,128)(2,1)} %param.20) | copy-start | bytes 196612
  429.4 134.5 %copy-start.2 = (f32[256,256]{1,0:T(8,128)S(1)}, f32[256,256]{1,0:T(8,128)}, u32[]{:S(2)}) copy-start(f32[256,256]{1,0:T(8,128)} %reduce-scatter.4.cloned.1.call-done) | copy-start | bytes 786436
  429.4 459.3 %all-reduce.3.cloned.1.call-start = ((), (), s32[]{:S(2)}) async-start(), calls=%async_computation.9 | async-start | bytes 786432 | tf_op jit(solution)/shard_map/psum | solution.py:100
Sparse Core Ops, SparseCore 0:
  10.6 85.6 all-gather.3
  167.8 66.1 reduce-scatter.3
  235.9 37.2 all-gather.7
  276.2 81.5 all-gather.5
  361.5 199.2 reduce-scatter.7
  563.2 69.0 reduce-scatter.5
  638.4 250.2 all-reduce.2
where the time goes:
time: 900 us; the launch traced here: 899 us
  waiting for transfers between devices  688 us (76%)
  matrix products  147 us (16%)
  local copies, waits for them, and re-layouts  47.9 us (5%)
  between operations  14.8 us (2%)
    psum x1, waiting for transfers between devices, on_device(): first_grad = lax.psum(first_local, ('row', 'col'))  255 us
    reduce_scatter x1, waiting for transfers between devices, on_device(): lax.psum_scatter(grad_part, 'col', scatter_dimension=0, tiled=True)  131 us
    dot_general x12, matrix products, add_group(): jnp.einsum('tr,taw->raw', select, products, precision=HIGHEST)  99.3 us
    all_gather x1, waiting for transfers between devices, on_device(): gathered_x = lax.all_gather(node_features, 'col', axis=0, tiled=True)  86.8 us
    reduce_scatter x1, waiting for transfers between devices, on_device(): lax.psum_scatter(hidden_part, 'row', scatter_dimension=0, tiled=True)  67.1 us
    reduce_scatter x1, waiting for transfers between devices, on_device(): lax.psum_scatter(feature_part, 'row', scatter_dimension=0, tiled=True)  65.5 us
    all_gather x1, waiting for transfers between devices, on_device(): gathered_h = lax.all_gather(hidden_act, 'col', axis=0, tiled=True)  44.8 us
    dot_general x12, matrix products, add_group(): jnp.einsum(einsum_form, group_tiles, picked, preferred_element_type=jnp.f...  39.1 us
  transfers between devices with their start and end apart: 7, of which 7 were waited for; matrix products, arithmetic and copies ran while one was open for 13% of the time, Pallas kernels for 0%

commit v1 on v0

--- a/solution.py
+++ b/solution.py
@@ -97,7 +97,8 @@
     pre_grad = hidden_grad * (sigma * (1.0 + first_pre * (1.0 - sigma)))
     second_grad = lax.psum(second_local, ("row", "col"))
     first_local = jnp.dot(first_mean.T, pre_grad, precision=HIGHEST) * scale
-    first_grad = lax.psum(first_local, ("row", "col"))
+    o_now = lax.psum(first_local, "col")
+    first_grad = lax.psum(o_now, "row")
     return (output, first_grad, second_grad)
 
 

time: 900 us -> 1130 us (1.26)
  waiting for transfers between devices: 688 us -> 922 us
    psum x1 -> x3, waiting for transfers between devices: 255 us -> 446 us  [the longest x1 248 us: on_device(): second_grad = lax.psum(second_local, ('row', 'col'))]
    reduce_scatter x1, waiting for transfers between devices: 131 us -> 203 us  [on_device(): lax.psum_scatter(grad_part, 'col', scatter_dimension=0, tiled=True)]
    reduce_scatter x1, waiting for transfers between devices: 65.5 us -> 25.9 us  [on_device(): lax.psum_scatter(feature_part, 'row', scatter_dimension=0, tiled=True)]
    all_gather x1, waiting for transfers between devices: 44.8 us -> 84.3 us  [on_device(): gathered_h = lax.all_gather(hidden_act, 'col', axis=0, tiled=True)]
    all_gather x1, waiting for transfers between devices: 37 us -> 0.02 us  [on_device(): gathered_g = lax.all_gather(out_grad, 'row', axis=0, tiled=True)]
  transfers between devices with their start and end apart: 7 -> 9, of which waited for: 7 -> 8; matrix products, arithmetic and copies ran while one was open for 13% -> 17% of each run, Pallas kernels for 0% -> 0%
where the time goes in v1:
time: 1130 us
  waiting for transfers between devices  922 us (82%)
  matrix products  146 us (13%)
  local copies, waits for them, and re-layouts  48.7 us (4%)
  between operations  14.6 us (1%)
    psum x1, waiting for transfers between devices, on_device(): second_grad = lax.psum(second_local, ('row', 'col'))  248 us
    reduce_scatter x1, waiting for transfers between devices, on_device(): lax.psum_scatter(grad_part, 'col', scatter_dimension=0, tiled=True)  203 us
    psum x1, waiting for transfers between devices, on_device(): first_grad = lax.psum(o_now, 'row')  122 us
    dot_general x12, matrix products, add_group(): jnp.einsum('tr,taw->raw', select, products, precision=HIGHEST)  99.2 us
    all_gather x1, waiting for transfers between devices, on_device(): gathered_x = lax.all_gather(node_features, 'col', axis=0, tiled=True)  86 us
    all_gather x1, waiting for transfers between devices, on_device(): gathered_h = lax.all_gather(hidden_act, 'col', axis=0, tiled=True)  84.3 us
    psum x1, waiting for transfers between devices, on_device(): o_now = lax.psum(first_local, 'col')  75.7 us
    reduce_scatter x1, waiting for transfers between devices, on_device(): lax.psum_scatter(hidden_part, 'row', scatter_dimension=0, tiled=True)  75.7 us
  transfers between devices with their start and end apart: 9, of which 8 were waited for; matrix products, arithmetic and copies ran while one was open for 17% of the time, Pallas kernels for 0%

profile of v1, /device:TPU:1, one launch (start us, length us, event | category | flops | bytes accessed | tf_op | source)
XLA Modules:
  0.0 1133.1 jit_solution(2484465045678664248)
XLA Ops:
  7.2 0.7 all-gather.4.cloned.1.call-update
  8.0 0.7 all-gather.8.cloned.1.call-update
  8.7 0.8 slice_reduce_fusion
  9.5 0.1 reshape_squeeze.4
  10.3 86.0 %all-gather.4.cloned.1.call-done = bf16[4096,256]{1,0:T(8,128)(2,1)} async-done(((bf16[256,256]{1,0:T(8,128)(2,1)}), bf16[4096,256]{1,0:T(8,128)(2,1)}) %all-gather.4.cloned.1.call-update) | async-done | bytes 2097168 | tf_op jit(solution)/shard_map/all_gather | solution.py:55
  96.3 64.6 %while.33 = (s32[]{:T(128)}, f32[32,128,256]{2,0,1:T(8,128)}, s32[4,32]{1,0:T(4,128)S(1)}, pred[4,32]{1,0:T(4,128)(4,1)S(1)}, bf16[4,32,128,128]{3,2,1,0:T(8,128...) while((s32[]{:T(128)}, f32[32,128,256]{2,0,1:T(8,128)}, ...), condition=%wide.region_1.3_spmd.clone, body=%wide.region_0.2_spmd.clone.sunk | while | flops 674237632 | bytes 24123028 | solution.py:34
  96.4 2.3 gather_fusion
  98.6 4.0 fusion.96
  102.6 8.9 select_add_fusion.6
  111.6 2.3 gather_fusion
  113.8 4.0 fusion.96
  117.8 10.2 select_add_fusion.6
  128.1 2.3 gather_fusion
  130.3 4.0 fusion.96
  134.3 10.2 select_add_fusion.6
  144.5 2.3 gather_fusion
  146.8 4.0 fusion.96
  150.8 10.2 select_add_fusion.6
  161.0 6.6 copy.10
  167.6 0.2 reduce-scatter.8.cloned.1.call-start
  167.8 35.7 %while.35 = (s32[]{:T(128)}, f32[32,128,128]{2,0,1:T(8,128)}, s32[4,32]{1,0:T(4,128)S(1)}, pred[4,32]{1,0:T(4,128)(4,1)S(1)}, bf16[4,32,128,128]{3,2,1,0:T(8,128...) while((s32[]{:T(128)}, f32[32,128,128]{2,0,1:T(8,128)}, ...), condition=%wide.region_7.9_spmd.clone, body=%wide.region_6.8_spmd.clone.sunk | while | flops 337120544 | bytes 12588823 | solution.py:34
  167.9 2.0 gather_fusion.2
  169.9 1.8 fusion.109
  171.7 3.8 select_add_fusion.8
  175.6 2.0 gather_fusion.2
  177.6 1.8 fusion.109
  179.4 5.5 select_add_fusion.8
  184.9 2.0 gather_fusion.2
  186.9 1.8 fusion.109
  188.8 5.5 select_add_fusion.8
  194.3 2.0 gather_fusion.2
  196.3 1.8 fusion.109
  198.1 5.4 select_add_fusion.8
  203.6 4.2 copy.12
  207.8 25.9 %reduce-scatter.4.cloned.1.call-done = f32[256,256]{1,0:T(8,128)} async-done(((f32[4096,256]{1,0:T(8,128)}), f32[256,256]{1,0:T(8,128)}) %reduce-scatter.4.cloned.1.call-update) | async-done | bytes 262160 | tf_op jit(solution)/shard_map/reduce_scatter | solution.py:65
  233.8 1.9 multiply_convert_fusion
  235.8 202.9 %reduce-scatter.8.cloned.1.call-done = f32[256,128]{1,0:T(8,128)} async-done(((f32[4096,128]{1,0:T(8,128)}), f32[256,128]{1,0:T(8,128)}) %reduce-scatter.8.cloned.1.call-update) | async-done | bytes 131088 | tf_op jit(solution)/shard_map/reduce_scatter | solution.py:92
  438.7 1.2 convolution_multiply_fusion.1
  439.9 2.3 convolution_multiply_fusion
  442.1 0.3 reduce-scatter.6.cloned.1.call-start
  442.4 84.3 %all-gather.6.cloned.1.call-done = bf16[4096,256]{1,0:T(8,128)(2,1)} async-done(((bf16[256,256]{1,0:T(8,128)(2,1)}), bf16[4096,256]{1,0:T(8,128)(2,1)}) %all-gather.6.cloned.1.call-update) | async-done | bytes 2097168 | tf_op jit(solution)/shard_map/all_gather | solution.py:69
  526.7 64.7 %while.34 = (s32[]{:T(128)}, f32[32,128,256]{2,0,1:T(8,128)}, s32[4,32]{1,0:T(4,128)S(1)}, pred[4,32]{1,0:T(4,128)(4,1)S(1)}, bf16[4,32,128,128]{3,2,1,0:T(8,128...) while((s32[]{:T(128)}, f32[32,128,256]{2,0,1:T(8,128)}, ...), condition=%wide.region_4.6_spmd.clone, body=%wide.region_3.5_spmd.clone.sunk | while | flops 674237632 | bytes 24123028 | solution.py:34
  526.8 2.3 gather_fusion.1
  529.0 4.0 fusion.102
  533.0 8.9 select_add_fusion.7
  542.0 2.3 gather_fusion.1
  544.2 4.0 fusion.102
  548.2 10.2 select_add_fusion.7
  558.5 2.3 gather_fusion.1
  560.7 4.0 fusion.102
  564.7 10.2 select_add_fusion.7
  574.9 2.3 gather_fusion.1
  577.2 4.0 fusion.102
  581.2 10.2 select_add_fusion.7
  591.4 6.6 copy.11
  598.1 0.8 copy-done.1
  599.0 1.0 convolution_multiply_fusion.2
  600.0 75.7 %all-reduce.4.cloned.1.call-done = f32[256,256]{1,0:T(8,128)} async-done(((f32[256,256]{1,0:T(8,128)}), f32[256,256]{1,0:T(8,128)}) %all-reduce.4.cloned.1.call-update) | async-done | bytes 262160 | tf_op jit(solution)/shard_map/psum | solution.py:100
  675.8 75.7 %reduce-scatter.6.cloned.1.call-done = f32[256,256]{1,0:T(8,128)} async-done(((f32[4096,256]{1,0:T(8,128)}), f32[256,256]{1,0:T(8,128)}) %reduce-scatter.6.cloned.1.call-update) | async-done | bytes 262160 | tf_op jit(solution)/shard_map/reduce_scatter | solution.py:79
  751.4 1.9 convolution_convert_fusion
  753.3 248.0 %all-reduce.8.cloned.1.call-done = f32[256,128]{1,0:T(8,128)} async-done(((f32[256,128]{1,0:T(8,128)}), f32[256,128]{1,0:T(8,128)}) %all-reduce.8.cloned.1.call-update) | async-done | bytes 131088 | tf_op jit(solution)/shard_map/psum | solution.py:98
  1001.3 122.0 %all-reduce.6.cloned.1.call-done = f32[256,256]{1,0:T(8,128)} async-done(((f32[256,256]{1,0:T(8,128)}), f32[256,256]{1,0:T(8,128)}) %all-reduce.6.cloned.1.call-update) | async-done | bytes 262160 | tf_op jit(solution)/shard_map/psum | solution.py:101
  1123.4 1.7 copy.56
  1125.0 1.6 copy.57
  (79 shorter events, 1.0 us)
Async XLA Ops:
  7.2 226.6 %copy-start = (bf16[256,256]{1,0:T(8,128)(2,1)S(1)}, bf16[256,256]{1,0:T(8,128)(2,1)}, u32[]{:S(2)}) copy-start(bf16[256,256]{1,0:T(8,128)(2,1)} %param.19) | copy-start | bytes 393220
  7.2 89.2 %all-gather.4.cloned.1.call-start = ((), (), s32[]{:S(2)}) async-start(), calls=%async_computation.3 | async-start | bytes 2228224 | tf_op jit(solution)/shard_map/all_gather | solution.py:55
  7.9 159.9 %all-gather.8.cloned.1.call-start = ((), (), s32[]{:S(2)}) async-start(), calls=%async_computation.7 | async-start | bytes 1114112 | tf_op jit(solution)/shard_map/all_gather | solution.py:82
  8.7 225.1 %reduce-scatter.4.cloned.1.call-start = ((), (), s32[]{:S(2)}) async-start(), calls=%async_computation.4 | async-start | bytes 4456448 | tf_op jit(solution)/shard_map/reduce_scatter | solution.py:65
  167.6 271.1 %reduce-scatter.8.cloned.1.call-start = ((), (), s32[]{:S(2)}) async-start(), calls=%async_computation.8 | async-start | bytes 2228224 | tf_op jit(solution)/shard_map/reduce_scatter | solution.py:92
  203.6 235.1 %copy-start.3 = (bf16[256,128]{1,0:T(8,128)(2,1)S(1)}, bf16[256,128]{1,0:T(8,128)(2,1)}, u32[]{:S(2)}) copy-start(bf16[256,128]{1,0:T(8,128)(2,1)} %param.20) | copy-start | bytes 196612
  207.8 318.9 %all-gather.6.cloned.1.call-start = ((), (), s32[]{:S(2)}) async-start(), calls=%async_computation.5 | async-start | bytes 2228224 | tf_op jit(solution)/shard_map/all_gather | solution.py:69
  235.7 440.0 %all-reduce.4.cloned.1.call-start = ((), (), s32[]{:S(2)}) async-start(), calls=%async_computation.9 | async-start | bytes 524288 | tf_op jit(solution)/shard_map/psum | solution.py:100
  442.1 309.3 %reduce-scatter.6.cloned.1.call-start = ((), (), s32[]{:S(2)}) async-start(), calls=%async_computation.6 | async-start | bytes 4456448 | tf_op jit(solution)/shard_map/reduce_scatter | solution.py:79
  598.0 0.9 copy-start.1
  598.0 1.0 copy-start.2
  598.0 403.3 %all-reduce.8.cloned.1.call-start = ((), (), s32[]{:S(2)}) async-start(), calls=%async_computation.11 | async-start | bytes 262144 | tf_op jit(solution)/shard_map/psum | solution.py:98
  599.9 523.4 %all-reduce.6.cloned.1.call-start = ((), (), s32[]{:S(2)}) async-start(), calls=%async_computation.10 | async-start | bytes 524288 | tf_op jit(solution)/shard_map/psum | solution.py:101
Sparse Core Ops, SparseCore 0:
  10.6 85.6 all-gather.3
  98.2 35.5 all-gather.7
  167.7 66.0 reduce-scatter.3
  237.5 201.1 reduce-scatter.7
  441.7 85.0 all-gather.5
  529.8 145.9 all-reduce.3
  678.4 72.9 reduce-scatter.5
  758.4 242.8 all-reduce.7
  1004.1 119.1 all-reduce.5
